TPU v7x, 32 devices: a whole 2x2x4 slice. The times are simulated.
32 devices in a mesh: groups: 2 (over y), item: 4 (over z), dp: 2 (over core), tensor: 2 (over x).
Axes of the slice: x: 2, y: 2, z: 4, core: 2. Of those that a mesh axis runs over, the one named last changes fastest.
Arguments:
- events: bfloat16 [12288, 1024], P(('groups', 'item', 'dp')), parts along dimension 0, may hold values from -6 to 6
- lengths: int32 [16], P('groups'), parts along dimension 0, may hold values from 192 to 768, as said below
- packing: int32 [16], P('groups'), parts along dimension 0, may hold values from 0 to 7, each once
- positions: int32 [16, 64], P('groups'), parts along dimension 0, may hold values from 0 to 767, as said below
- logged: int32 [16, 64], P('groups'), parts along dimension 0, may hold values from 0 to 16383
- w_uvqk: bfloat16 [1024, 1024], P(None, 'tensor'), may hold values from -0.1875 to 0.1875
- w_out: bfloat16 [256, 1024], P('tensor'), may hold values from -0.375 to 0.375
- catalogue: bfloat16 [16384, 1024], P(('item', 'dp', 'tensor')), may hold values from -0.46875 to 0.46875
Outputs:
- scoring_state: bfloat16 [1024, 1024], P(('groups', 'item', 'dp'), 'tensor'), parts along dimension 0
- log_propensity: float32 [1024], P(('groups', 'item', 'dp')), parts along dimension 0
There are 2 independent parts, one for each index of `groups`. A program takes and returns all parts, laid end to end along the dimension named above; an argument that names none is the same for every part. Nothing has to cross between parts.
Inputs may be any that keep to these rules, and one draw needn't show every extreme that they name: `lengths`: one history has exactly 768 valid events and one exactly 192. positions[h, k] < lengths[h]. `packing`: each history id appears once.
All inputs are finite; a program needn't handle non-finite values.
Results may differ from a plain program's by a relative error of at most 0.0048.
Values may be sent and summed in bfloat16 or wider, within the bound.
A program may use at most 64 MiB of HBM per device.

v0:
```python
import math

import jax
import jax.numpy as jnp
from jax import lax
from jax.sharding import PartitionSpec as P

DH = 128


def pick_target(logits, item_ids, item_base):
    local_ids = item_ids - item_base
    matches = jnp.arange(logits.shape[1], dtype=jnp.int32)[None, :] == local_ids[:, None]
    return jnp.sum(jnp.where(matches, logits, 0.0), axis=1)


def local(events, lengths, packing, positions, logged, w_uvqk, w_out, catalogue):
    slot_rows, model_width = events.shape
    hist_count = packing.shape[0]
    imp_count = positions.shape[1]
    local_heads = w_out.shape[0] // DH
    item_count = catalogue.shape[0]
    slot_index = lax.axis_index(("item", "dp"))
    hist_ids = jnp.arange(hist_count, dtype=jnp.int32)
    slot_pick = (packing[:, None] == hist_ids[None, :]).astype(jnp.int32)
    owned = (hist_ids == slot_index).astype(jnp.int32)
    hist_row = jnp.sum(slot_pick * owned[:, None], axis=0)
    hist_length = jnp.sum(hist_row * lengths)
    event_spots = jnp.sum(hist_row[:, None] * positions, axis=0)
    slot_items = jnp.sum(slot_pick[:, :, None] * logged[None, :, :], axis=1).reshape(
        hist_count * imp_count
    )
    item_base = lax.axis_index(("item", "dp", "tensor")) * item_count
    split_weights = w_uvqk.reshape(model_width, local_heads, 4, DH)
    w_values_keys = split_weights[:, :, 1::2].reshape(model_width, local_heads * 2 * DH)
    w_gate_query = split_weights[:, :, 0::2].reshape(model_width, local_heads * 2 * DH)
    values_keys = jnp.dot(events, w_values_keys, preferred_element_type=jnp.float32)
    values_keys = (
        jax.nn.silu(values_keys).astype(jnp.bfloat16).reshape(slot_rows, local_heads, 2, DH)
    )
    chosen = jnp.take(events, event_spots, axis=0)
    gate_query = jnp.dot(chosen, w_gate_query, preferred_element_type=jnp.float32)
    gate_query = jax.nn.silu(gate_query).astype(jnp.bfloat16).reshape(imp_count, local_heads, 2, DH)
    scores = jnp.einsum(
        "ied,med->iem",
        gate_query[:, :, 1],
        values_keys[:, :, 1],
        preferred_element_type=jnp.float32,
    ) / math.sqrt(DH)
    slot_range = jnp.arange(slot_rows, dtype=jnp.int32)
    is_valid = (slot_range[None, :] <= event_spots[:, None]) & (slot_range[None, :] < hist_length)
    weights = jnp.where(is_valid[:, None, :], jax.nn.silu(scores), 0.0).astype(jnp.bfloat16)
    attended = jnp.einsum(
        "iem,med->ied", weights, values_keys[:, :, 0], preferred_element_type=jnp.float32
    )
    inverse = lax.rsqrt(jnp.mean(attended * attended, axis=-1, keepdims=True) + 1e-06)
    gated_rows = (attended * inverse * gate_query[:, :, 0].astype(jnp.float32)).astype(jnp.bfloat16)
    gated_rows = gated_rows.reshape(imp_count, local_heads * DH)
    partial_out = jnp.dot(gated_rows, w_out, preferred_element_type=jnp.float32)
    residual = chosen.astype(jnp.float32)
    col_share = model_width // lax.axis_size("tensor")
    col_start = lax.axis_index("tensor") * col_share
    summed = lax.psum(partial_out, "tensor")
    hidden_state = (summed + residual).astype(jnp.bfloat16)
    state_out = lax.dynamic_slice_in_dim(hidden_state, col_start, col_share, 1)
    logits = lax.dot_general(
        lax.all_gather(hidden_state, ("item", "dp"), axis=0, tiled=True),
        catalogue,
        (((1,), (1,)), ((), ())),
        preferred_element_type=jnp.float32,
    )
    new_totals = jnp.sum(jnp.exp(logits), axis=1)
    new_target = pick_target(logits, slot_items, item_base)
    whole_totals, whole_target = lax.psum((new_totals, new_target), ("item", "dp", "tensor"))
    mine_totals = lax.dynamic_slice_in_dim(whole_totals, slot_index * imp_count, imp_count, 0)
    mine_target = lax.dynamic_slice_in_dim(whole_target, slot_index * imp_count, imp_count, 0)
    return (state_out, mine_target - jnp.log(mine_totals))


def solution(mesh):
    placed = (
        P(("groups", "item", "dp"), None),
        P("groups"),
        P("groups"),
        P("groups", None),
        P("groups", None),
        P(None, "tensor"),
        P("tensor", None),
        P(("item", "dp", "tensor"), None),
    )
    return jax.shard_map(
        local,
        mesh=mesh,
        in_specs=placed,
        out_specs=(P(("groups", "item", "dp"), "tensor"), P(("groups", "item", "dp"))),
        check_vma=False,
    )
```

profile of v0, /device:TPU:0, one launch (start us, length us, event | category | flops | bytes accessed | tf_op | source)
XLA Modules:
  0.0 136.1 jit_solution(11309855949234600494)
XLA Ops:
  7.2 0.0 copy-start
  7.2 0.0 all-reduce.3.cloned.1.call-start
  7.2 0.9 select_reduce_fusion.1
  8.1 0.8 multiply_reduce_fusion.2
  8.9 1.3 reshape.175
  10.3 0.0 copy-start.5
  10.3 12.4 %slice.21 = bf16[1024,1,2,128]{3,2,0,1:T(2,128)(2,1)} slice(bf16[1024,1,4,128]{3,2,0,1:T(4,128)(2,1)S(1)} %reshape.175), slice={[0:1024:1], [0:1:1], [0:4:2], [0:128:1]} | slice | bytes 1048576 | tf_op jit(solution)/shard_map/slice | solution.py:36
  22.6 12.4 %slice.18 = bf16[1024,1,2,128]{3,2,0,1:T(2,128)(2,1)} slice(bf16[1024,1,4,128]{3,2,0,1:T(4,128)(2,1)S(1)} %reshape.175), slice={[0:1024:1], [0:1:1], [1:4:2], [0:128:1]} | slice | bytes 1048576 | tf_op jit(solution)/shard_map/slice | solution.py:35
  35.0 2.5 %gather_fusion = bf16[64,1024]{1,0:T(8,128)(2,1)S(1)} fusion(bf16[768,1024]{1,0:T(8,128)(2,1)} %param.8, s32[1024]{0:T(1024)S(1)} %pad_clamp_fusion), kind=kCustom, calls=%fused_computation | custom fusion | bytes 262400 | tf_op jit(solution)/shard_map/jit(_take)/gather | solution.py:41
  37.5 1.3 multiply_convert_fusion.1
  38.8 0.1 fusion.30
  38.9 0.6 multiply_reduce_fusion.3
  39.5 0.6 iota_compare_fusion.2
  40.2 0.0 copy-start.2
  40.2 2.1 %multiply_convert_fusion = bf16[768,256]{0,1:T(8,128)(2,1)S(1)} fusion(bf16[768,1024]{1,0:T(8,128)(2,1)} %param.8, bf16[128,8,2,128]{3,2,1,0:T(2,128)(2,1)S(1)} %bitcast.81), kind=kOutput, calls=%fused_computation.7 | convolution fusion | flops 403636224 | bytes 2490368 | tf_op jit(solution)/shard_map/dot_general | solution.py:37
  42.4 0.0 copy-start.4
  42.4 0.0 copy-start.3
  42.4 0.4 multiply_reduce_fusion.1
  42.8 0.9 fusion.21
  43.8 0.0 all-reduce.3.cloned.1.call-update
  43.8 0.0 all-gather.2.cloned.1.call-start
  43.9 26.0 %all-reduce.3.cloned.1.call-done = f32[64,1024]{1,0:T(8,128)} async-done(((f32[64,1024]{1,0:T(8,128)}), f32[64,1024]{1,0:T(8,128)}) %all-reduce.3.cloned.1.call-update) | async-done | bytes 262160 | tf_op jit(solution)/shard_map/psum | solution.py:63
  69.8 1.7 %add_convert_fusion = bf16[64,1024]{1,0:T(8,128)(2,1)} fusion(f32[64,1024]{1,0:T(8,128)} %all-reduce.3.cloned.1.call-done, bf16[64,1024]{1,0:T(8,128)(2,1)S(1)} %gather_fusion, pred[64]{0:T(512)(128)(4,1)S(1)} %compare_and_fusion), kind=kLoop, calls=%fused_computation.14 | loop fusion | flops 262144 | bytes 524352 | tf_op jit(solution)/shard_map/convert_element_type | solution.py:64
  71.5 0.0 all-gather.2.cloned.1.call-update
  71.6 0.1 fusion.24
  71.7 0.1 multiply_reduce_fusion
  71.8 0.1 sub.18
  71.8 1.5 %constant_dynamic-slice_fusion = bf16[64,512]{1,0:T(8,128)(2,1)} fusion(bf16[64,1024]{1,0:T(8,128)(2,1)} %add_convert_fusion, s32[]{:T(128)S(6)} %select_n.39), kind=kLoop, calls=%fused_computation.52 | loop fusion | bytes 131076 | tf_op jit(solution)/shard_map/dynamic_slice | solution.py:65
  73.3 20.5 %all-gather.2.cloned.1.call-done = bf16[512,1024]{1,0:T(8,128)(2,1)} async-done(((bf16[64,1024]{1,0:T(8,128)(2,1)}), bf16[512,1024]{1,0:T(8,128)(2,1)}) %all-gather.2.cloned.1.call-update) | async-done | bytes 1048592 | tf_op jit(solution)/shard_map/all_gather | solution.py:67
  93.8 2.8 %select_reduce_fusion = (f32[512]{0:T(512)S(1)}, f32[512]{0:T(512)S(1)}) fusion(s32[512]{0:T(512)S(1)} %sub.18, bf16[512,1024]{1,0:T(8,128)(2,1)} %all-gather.2.cloned.1.call-done, bf16[1024,1024]{1,0:T(8,128)(2,1)S(1)} %copy-done), kind=kOutput, calls=%fused_computation.2 | convolution fusion | flops 1075837952 | bytes 3151872 | tf_op jit(solution)/shard_map/dot_general | solution.py:66
  96.6 32.1 %all-reduce = (f32[512]{0:T(512)S(1)}, f32[512]{0:T(512)S(1)}) all-reduce(f32[512]{0:T(512)S(1)} %get-tuple-element.3, f32[512]{0:T(512)S(1)} %get-tuple-element.2), channel_id=1, replica_groups=mesh['groups'=2,'item'=4,'dp'=2,'tensor'=2] {'item','dp','tensor'}, use_global_device_ids=true, to_apply=%region_9.10 | all-reduce | flops 1024 | bytes 8192 | tf_op jit(solution)/shard_map/psum | solution.py:74
  128.7 0.6 log_subtract_fusion
  (14 shorter events, 0.1 us)
Async XLA Ops:
  7.2 86.7 %copy-start = (bf16[1024,1024]{1,0:T(8,128)(2,1)S(1)}, bf16[1024,1024]{1,0:T(8,128)(2,1)}, u32[]{:S(2)}) copy-start(bf16[1024,1024]{1,0:T(8,128)(2,1)} %param.15) | copy-start | bytes 6291460
  7.2 62.7 %all-reduce.3.cloned.1.call-start = ((), (), s32[]{:S(2)}) async-start(), calls=%async_computation | async-start | bytes 524288 | tf_op jit(solution)/shard_map/psum | solution.py:63
  10.3 28.6 %copy-start.5 = (s32[8]{0:T(128)S(1)}, s32[8]{0:T(128)}, u32[]{:S(2)}) copy-start(s32[8]{0:T(128)} %param.9) | copy-start | bytes 100
  35.0 5.2 %copy-start.1 = (bf16[1024,1,2,128]{3,2,0,1:T(2,128)(2,1)S(1)}, bf16[1024,1,2,128]{3,2,0,1:T(2,128)(2,1)}, u32[]{:S(2)}) copy-start(bf16[1024,1,2,128]{3,2,0,1:T(2,128)(2,1)} %slice.18) | copy-start | bytes 1572868
  40.2 2.6 %copy-start.2 = (bf16[128,1024]{1,0:T(8,128)(2,1)S(1)}, bf16[128,1024]{1,0:T(8,128)(2,1)}, u32[]{:S(2)}) copy-start(bf16[128,1024]{1,0:T(8,128)(2,1)} %param.14) | copy-start | bytes 786436
  42.4 29.2 %copy-start.4 = (s32[8]{0:T(128)S(1)}, s32[8]{0:T(128)}, u32[]{:S(2)}) copy-start(s32[8]{0:T(128)} %param.10) | copy-start | bytes 100
  42.4 29.3 %copy-start.3 = (s32[8,64]{1,0:T(8,128)S(1)}, s32[8,64]{1,0:T(8,128)}, u32[]{:S(2)}) copy-start(s32[8,64]{1,0:T(8,128)} %param.12) | copy-start | bytes 6148
  43.8 50.0 %all-gather.2.cloned.1.call-start = ((), (), s32[]{:S(2)}) async-start(), calls=%async_computation.1 | async-start | bytes 1179648 | tf_op jit(solution)/shard_map/all_gather | solution.py:67
Sparse Core Ops, SparseCore 0:
  43.9 25.8 all-reduce.2
  71.7 22.0 all-gather.1
where the time goes:
time: 137 us; the launch traced here: 136 us
  waiting for transfers between devices  46.5 us (34%)
  blocking collectives  32.1 us (23%)
  local copies, waits for them, and re-layouts  30.2 us (22%)
  between operations  14.2 us (10%)
  matrix products  7.63 us (6%)
  other arithmetic  5.41 us (4%)
    psum x1, blocking collectives, local(): lax.psum((new_totals, new_target), ('item', 'dp', 'tensor'))  32.1 us
    psum x1, waiting for transfers between devices, local(): summed = lax.psum(partial_out, 'tensor')  26 us
    all_gather x1, waiting for transfers between devices, local(): lax.all_gather(hidden_state, ('item', 'dp'), axis=0, tiled=True)  20.5 us
    slice x1, local copies, waits for them, and re-layouts, local(): split_weights[:, :, 1::2].reshape(model_width, local_heads * 2 * DH)  12.4 us
    slice x1, local copies, waits for them, and re-layouts, local(): split_weights[:, :, 0::2].reshape(model_width, local_heads * 2 * DH)  12.4 us
    dot_general x1, matrix products, local(): lax.dot_general(lax.all_gather(hidden_state, ('item', 'dp'), axis=0, tile...  2.82 us
  transfers between devices with their start and end apart: 2, of which 2 were waited for; matrix products, arithmetic and copies ran while one was open for 1% of the time, Pallas kernels for 0%

commit v1 on v0

v1 whole, which is shorter than its diff:
```python
import functools
import math

import jax
import jax.numpy as jnp
from jax import lax
from jax.experimental import pallas as pl
from jax.experimental.pallas import tpu as pltpu
from jax.sharding import PartitionSpec as P

DH = 128
LANES = 128
ITEM_BLOCK = 256
MESH = pl.DeviceIdType.MESH


def silu(x):
    return x / (1.0 + jnp.exp(-x))


def kernel(
    nz,
    nt,
    packing,
    lengths,
    positions,
    logged,
    events_hbm,
    w_hbm,
    w_out_hbm,
    cat_hbm,
    state_out,
    prop_out,
    events,
    w_vk,
    w_uq,
    w_full,
    cat,
    chosen_all,
    gated_all,
    states,
    ids,
    stage,
    stats,
    load_sem,
    z_send,
    z_recv,
    sib_send,
    sib_recv,
    g_send,
    g_recv,
    gs_send,
    gs_recv,
    w_send,
    w_recv,
    s_send,
    s_recv,
):
    z = lax.axis_index("item")
    c = lax.axis_index("dp")
    t = lax.axis_index("tensor")
    slot = z * 2 + c
    imps = positions.shape[1]
    rows, width = events.shape
    nslots = nz * 2
    nlines = nz * nt
    ndev = nlines * 2
    line = z * nt + t
    me = slot * nt + t

    def device(lin):
        peer_slot = lin // nt
        return {"item": peer_slot // 2, "dp": lax.rem(peer_slot, 2), "tensor": lax.rem(lin, nt)}

    loads = [
        pltpu.make_async_copy(events_hbm, events, load_sem.at[0]),
        pltpu.make_async_copy(w_hbm.at[:, 0:DH], w_uq.at[:, 0:DH], load_sem.at[1]),
        pltpu.make_async_copy(w_hbm.at[:, 2 * DH : 3 * DH], w_uq.at[:, DH : 2 * DH], load_sem.at[2]),
        pltpu.make_async_copy(w_hbm.at[:, DH : 2 * DH], w_vk.at[:, 0:DH], load_sem.at[3]),
        pltpu.make_async_copy(w_hbm.at[:, 3 * DH : 4 * DH], w_vk.at[:, DH : 2 * DH], load_sem.at[4]),
        pltpu.make_async_copy(w_out_hbm, w_full.at[pl.ds(pl.multiple_of(t * DH, DH), DH), :], load_sem.at[5]),
        pltpu.make_async_copy(cat_hbm, cat, load_sem.at[6]),
    ]
    for copy in loads:
        copy.start()

    barrier = pltpu.get_barrier_semaphore()

    def greet(r, carry):
        pl.semaphore_signal(
            barrier, inc=1, device_id=device(lax.rem(me + r, ndev)), device_id_type=MESH
        )
        return carry

    lax.fori_loop(1, ndev, greet, 0)

    hist = packing[slot]
    length = lengths[hist].astype(jnp.float32)
    pos_row = positions[pl.ds(hist, 1), :].astype(jnp.float32)
    eye = lax.broadcasted_iota(jnp.int32, (imps, imps), 0) == lax.broadcasted_iota(
        jnp.int32, (imps, imps), 1
    )
    pos_col = jnp.sum(jnp.where(eye, pos_row, 0.0), axis=1, keepdims=True)
    spots = lax.broadcasted_iota(jnp.int32, (imps, rows), 1).astype(jnp.float32)
    pick = jnp.where(spots == pos_col, 1.0, 0.0).astype(jnp.bfloat16)
    for j in range(nslots):
        ids[0:1, j * imps : (j + 1) * imps] = logged[pl.ds(packing[j], 1), :]

    def rows_of(which):
        return pl.ds(pl.multiple_of(which * imps, imps), imps)

    loads[0].wait()
    chosen = jnp.dot(pick, events[...], preferred_element_type=jnp.float32).astype(jnp.bfloat16)
    chosen_all[rows_of(slot), :] = chosen
    pl.semaphore_wait(barrier, ndev - 1)

    def z_copy(r, source_slot):
        return pltpu.make_async_remote_copy(
            src_ref=chosen_all.at[rows_of(source_slot), :],
            dst_ref=chosen_all.at[rows_of(source_slot), :],
            send_sem=z_send.at[r],
            recv_sem=z_recv.at[r],
            device_id={"item": lax.rem(z + r, nz)},
            device_id_type=MESH,
        )

    def sib_copy(r, source_slot):
        return pltpu.make_async_remote_copy(
            src_ref=chosen_all.at[rows_of(source_slot), :],
            dst_ref=chosen_all.at[rows_of(source_slot), :],
            send_sem=sib_send.at[r],
            recv_sem=sib_recv.at[r],
            device_id={"dp": 1 - c},
            device_id_type=MESH,
        )

    def head_cols(which):
        return pl.ds(pl.multiple_of(which * DH, DH), DH)

    def w_copy(r, source_t):
        return pltpu.make_async_remote_copy(
            src_ref=w_out_hbm,
            dst_ref=w_full.at[head_cols(source_t), :],
            send_sem=w_send.at[r],
            recv_sem=w_recv.at[r],
            device_id={"tensor": lax.rem(t + r, nt)},
            device_id_type=MESH,
        )

    def gated_at(source_slot, source_t):
        return gated_all.at[rows_of(source_slot), head_cols(source_t)]

    def g_copy(r, source_slot, source_t):
        peer = lax.rem(line + r, nlines)
        return pltpu.make_async_remote_copy(
            src_ref=gated_at(source_slot, source_t),
            dst_ref=gated_at(source_slot, source_t),
            send_sem=g_send.at[r],
            recv_sem=g_recv.at[r],
            device_id={"item": peer // nt, "tensor": lax.rem(peer, nt)},
            device_id_type=MESH,
        )

    def gs_copy(r, source_slot, source_t):
        return pltpu.make_async_remote_copy(
            src_ref=gated_at(source_slot, source_t),
            dst_ref=gated_at(source_slot, source_t),
            send_sem=gs_send.at[r],
            recv_sem=gs_recv.at[r],
            device_id={"dp": 1 - c},
            device_id_type=MESH,
        )

    def loop(first, count, body):
        def step(r, carry):
            body(r)
            return carry

        lax.fori_loop(first, count, step, 0)

    loop(1, nz, lambda r: z_copy(r, slot).start())
    sib_copy(0, slot).start()
    loop(1, nt, lambda r: w_copy(r, t).start())

    loads[1].wait()
    loads[2].wait()
    gate_query = silu(
        jnp.dot(chosen, w_uq[...], preferred_element_type=jnp.float32)
    ).astype(jnp.bfloat16)
    loads[3].wait()
    loads[4].wait()
    values_keys = silu(
        jnp.dot(events[...], w_vk[...], preferred_element_type=jnp.float32)
    ).astype(jnp.bfloat16)
    scores = lax.dot_general(
        gate_query[:, DH:],
        values_keys[:, DH:],
        (((1,), (1,)), ((), ())),
        preferred_element_type=jnp.float32,
    ) * (1.0 / math.sqrt(DH))
    is_valid = (spots <= pos_col) & (spots < length)
    weights = jnp.where(is_valid, silu(scores), 0.0).astype(jnp.bfloat16)
    attended = jnp.dot(weights, values_keys[:, :DH], preferred_element_type=jnp.float32)
    inverse = lax.rsqrt(jnp.mean(attended * attended, axis=-1, keepdims=True) + 1e-06)
    gated = (attended * inverse * gate_query[:, :DH].astype(jnp.float32)).astype(jnp.bfloat16)
    gated_all[rows_of(slot), head_cols(t)] = gated

    loop(1, nlines, lambda r: g_copy(r, slot, t).start())
    gs_copy(0, slot, t).start()

    def z_source(r):
        return lax.rem(z + nz - r, nz) * 2

    def pass_chosen(r):
        z_copy(r, z_source(r) + c).wait_recv()
        sib_copy(r, z_source(r) + c).start()

    loop(1, nz, pass_chosen)

    def line_source(r):
        source = lax.rem(line + nlines - r, nlines)
        return (source // nt) * 2, lax.rem(source, nt)

    def pass_gated(r):
        base, source_t = line_source(r)
        g_copy(r, base + c, source_t).wait_recv()
        gs_copy(r, base + c, source_t).start()

    loop(1, nlines, pass_gated)

    loads[5].wait()
    loads[6].wait()
    loop(1, nt, lambda r: w_copy(r, lax.rem(t + nt - r, nt)).wait_recv())
    loop(0, nz, lambda r: sib_copy(r, z_source(r) + 1 - c).wait_recv())

    def take_gated(r):
        base, source_t = line_source(r)
        gs_copy(r, base + 1 - c, source_t).wait_recv()

    loop(0, nlines, take_gated)

    states[...] = (
        jnp.dot(gated_all[...], w_full[...], preferred_element_type=jnp.float32)
        + chosen_all[...].astype(jnp.float32)
    ).astype(jnp.bfloat16)
    share = width // nt
    state_out[...] = states[rows_of(slot), pl.ds(pl.multiple_of(t * share, LANES), share)]

    items = cat.shape[0]
    item_ids = ids[...]

    def block(b, carry):
        totals, target = carry
        logits = lax.dot_general(
            cat[pl.ds(pl.multiple_of(b * ITEM_BLOCK, ITEM_BLOCK), ITEM_BLOCK), :],
            states[...],
            (((1,), (1,)), ((), ())),
            preferred_element_type=jnp.float32,
        )
        local = item_ids - (me * items + b * ITEM_BLOCK)
        matches = lax.broadcasted_iota(jnp.int32, logits.shape, 0) == local
        totals = totals + jnp.sum(jnp.exp(logits), axis=0, keepdims=True)
        target = target + jnp.sum(jnp.where(matches, logits, 0.0), axis=0, keepdims=True)
        return totals, target

    zero = jnp.zeros((1, nslots * imps), jnp.float32)
    totals, target = lax.fori_loop(0, items // ITEM_BLOCK, block, (zero, zero))
    upper = lax.broadcasted_iota(jnp.int32, (8, LANES), 0) < 4
    for j in range(nz):
        cut = slice(j * LANES, (j + 1) * LANES)
        stage[j] = jnp.where(upper, totals[:, cut], target[:, cut])

    def s_copy(r, source):
        peer = lax.rem(me + r, ndev)
        return pltpu.make_async_remote_copy(
            src_ref=stage.at[peer // (2 * nt)],
            dst_ref=stats.at[source],
            send_sem=s_send.at[r],
            recv_sem=s_recv.at[r],
            device_id=device(peer),
            device_id_type=MESH,
        )

    loop(1, ndev, lambda r: s_copy(r, me).start())
    stats[me] = stage[z]

    loop(1, nz, lambda r: z_copy(r, slot).wait_send())
    loop(0, nz, lambda r: sib_copy(r, z_source(r) + c).wait_send())
    loop(1, nt, lambda r: w_copy(r, t).wait_send())
    loop(1, nlines, lambda r: g_copy(r, slot, t).wait_send())

    def sent_gated(r):
        base, source_t = line_source(r)
        gs_copy(r, base + c, source_t).wait_send()

    loop(0, nlines, sent_gated)
    loop(1, ndev, lambda r: s_copy(r, lax.rem(me + ndev - r, ndev)).wait_recv())
    whole = jnp.sum(stats[...], axis=0)
    prop = whole[4:5, :] - jnp.log(whole[0:1, :])
    prop = jnp.where(c == 0, prop, pltpu.roll(prop, LANES - imps, 1))
    prop_out[...] = prop[:, :imps]
    loop(1, ndev, lambda r: s_copy(r, me).wait_send())


def local(events, lengths, packing, positions, logged, w_uvqk, w_out, catalogue):
    rows, width = events.shape
    imps = positions.shape[1]
    nz = lax.axis_size("item")
    nt = lax.axis_size("tensor")
    nslots = nz * 2
    ndev = nslots * nt
    items = catalogue.shape[0]
    total_imps = nslots * imps
    dma = pltpu.SemaphoreType.DMA
    smem = pl.BlockSpec(memory_space=pltpu.SMEM)
    vmem = pl.BlockSpec(memory_space=pltpu.VMEM)
    hbm = pl.BlockSpec(memory_space=pl.ANY)
    state, prop = pl.pallas_call(
        functools.partial(kernel, nz, nt),
        out_shape=(
            jax.ShapeDtypeStruct((imps, width // nt), jnp.bfloat16),
            jax.ShapeDtypeStruct((1, imps), jnp.float32),
        ),
        in_specs=[smem, smem, vmem, vmem, hbm, hbm, hbm, hbm],
        out_specs=(vmem, vmem),
        scratch_shapes=[
            pltpu.VMEM((rows, width), jnp.bfloat16),
            pltpu.VMEM((width, 2 * DH), jnp.bfloat16),
            pltpu.VMEM((width, 2 * DH), jnp.bfloat16),
            pltpu.VMEM((nt * DH, width), jnp.bfloat16),
            pltpu.VMEM((items, width), jnp.bfloat16),
            pltpu.VMEM((total_imps, width), jnp.bfloat16),
            pltpu.VMEM((total_imps, nt * DH), jnp.bfloat16),
            pltpu.VMEM((total_imps, width), jnp.bfloat16),
            pltpu.VMEM((1, total_imps), jnp.int32),
            pltpu.VMEM((nz, 8, LANES), jnp.float32),
            pltpu.VMEM((ndev, 8, LANES), jnp.float32),
            dma((7,)),
            dma((nz,)),
            dma((nz,)),
            dma((nz,)),
            dma((nz,)),
            dma((nz * nt,)),
            dma((nz * nt,)),
            dma((nz * nt,)),
            dma((nz * nt,)),
            dma((nt,)),
            dma((nt,)),
            dma((ndev,)),
            dma((ndev,)),
        ],
        compiler_params=pltpu.CompilerParams(
            collective_id=0, has_side_effects=True, vmem_limit_bytes=48 * 1024 * 1024
        ),
        name="replay",
    )(packing, lengths, positions, logged, events, w_uvqk, w_out, catalogue)
    return state, prop.reshape(imps)


def solution(mesh):
    placed = (
        P(("groups", "item", "dp"), None),
        P("groups"),
        P("groups"),
        P("groups", None),
        P("groups", None),
        P(None, "tensor"),
        P("tensor", None),
        P(("item", "dp", "tensor"), None),
    )
    return jax.shard_map(
        local,
        mesh=mesh,
        in_specs=placed,
        out_specs=(P(("groups", "item", "dp"), "tensor"), P(("groups", "item", "dp"))),
        check_vma=False,
    )
```

time: 137 us -> 42 us (0.31)
  waiting for transfers between devices: 46.5 us -> 0 us
  blocking collectives: 32.1 us -> 0 us
  Pallas kernels: 0 us -> 32 us
  local copies, waits for them, and re-layouts: 30.2 us -> 8.99 us
  between operations: 14.2 us -> 0.66 us
  matrix products: 7.63 us -> 0 us
  other arithmetic: 5.41 us -> 0 us
    psum x1 -> x0, blocking collectives: 32.1 us -> none  [local(): lax.psum((new_totals, new_target), ('item', 'dp', 'tensor'))]
    pallas_call x0 -> x1, Pallas kernels: none -> 32 us  [local(): pl.pallas_call(functools.partial(kernel, nz, nt), out_shape=(jax.ShapeDty...]
    psum x1 -> x0, waiting for transfers between devices: 26 us -> none  [local(): summed = lax.psum(partial_out, 'tensor')]
    slice x3 -> x0, local copies, waits for them, and re-layouts: 24.8 us -> none  [the longest x1 12.4 us: local(): split_weights[:, :, 1::2].reshape(model_width, local_heads * 2 * DH)]
    all_gather x1 -> x0, waiting for transfers between devices: 20.5 us -> none  [local(): lax.all_gather(hidden_state, ('item', 'dp'), axis=0, tiled=True)]
    unnamed x12 -> x18, local copies, waits for them, and re-layouts: 0.04 us -> 8.99 us
    dot_general x5 -> x0, matrix products: 7.63 us -> none  [the longest x1 2.82 us: local(): lax.dot_general(lax.all_gather(hidden_state, ('item', 'dp'), axis=0, tile...]
    gather x1 -> x0, local copies, waits for them, and re-layouts: 2.47 us -> none  [local(): chosen = jnp.take(events, event_spots, axis=0)]
  transfers between devices with their start and end apart: 2 -> 0, of which waited for: 2 -> 0; matrix products, arithmetic and copies ran while one was open for 1% -> 0% of each run, Pallas kernels for 0% -> 0%
where the time goes in v1:
time: 42 us; the launch traced here: 41.7 us
  Pallas kernels  32 us (76%)
  local copies, waits for them, and re-layouts  8.99 us (21%)
  between operations  0.66 us (2%)
    pallas_call x1, Pallas kernels, local(): pl.pallas_call(functools.partial(kernel, nz, nt), out_shape=(jax.ShapeDty...  32 us
    unnamed x18, local copies, waits for them, and re-layouts  8.99 us

profile of v1, /device:TPU:0, one launch (start us, length us, event | category | flops | bytes accessed | tf_op | source)
XLA Modules:
  0.0 41.7 jit_solution(6540390138536256967)
XLA Ops:
  0.6 0.0 copy-start
  0.6 1.6 %copy-done = bf16[1024,1024]{1,0:T(8,128)(2,1)S(1)} copy-done((bf16[1024,1024]{1,0:T(8,128)(2,1)S(1)}, bf16[1024,1024]{1,0:T(8,128)(2,1)}, u32[]{:S(2)}) %copy-start) | copy-done | bytes 2097176
  2.2 0.0 copy-start.1
  2.2 1.4 %copy-done.1 = bf16[768,1024]{1,0:T(8,128)(2,1)S(1)} copy-done((bf16[768,1024]{1,0:T(8,128)(2,1)S(1)}, bf16[768,1024]{1,0:T(8,128)(2,1)}, u32[]{:S(2)}) %copy-start.1) | copy-done | bytes 1572888
  3.6 0.0 copy-start.2
  3.6 1.2 %copy-done.2 = bf16[1024,512]{1,0:T(8,128)(2,1)S(1)} copy-done((bf16[1024,512]{1,0:T(8,128)(2,1)S(1)}, bf16[1024,512]{1,0:T(8,128)(2,1)}, u32[]{:S(2)}) %copy-start.2) | copy-done | bytes 1048600
  4.9 0.0 copy-start.3
  4.9 0.9 %copy-done.3 = bf16[128,1024]{1,0:T(8,128)(2,1)S(1)} copy-done((bf16[128,1024]{1,0:T(8,128)(2,1)S(1)}, bf16[128,1024]{1,0:T(8,128)(2,1)}, u32[]{:S(2)}) %copy-start.3) | copy-done | bytes 262168
  5.8 0.0 copy-start.4
  5.8 0.7 %copy-done.4 = s32[8,64]{1,0:T(8,128)S(1)} copy-done((s32[8,64]{1,0:T(8,128)S(1)}, s32[8,64]{1,0:T(8,128)}, u32[]{:S(2)}) %copy-start.4) | copy-done | bytes 2072
  6.5 0.0 copy-start.5
  6.5 0.7 %copy-done.5 = s32[8,64]{1,0:T(8,128)S(1)} copy-done((s32[8,64]{1,0:T(8,128)S(1)}, s32[8,64]{1,0:T(8,128)}, u32[]{:S(2)}) %copy-start.5) | copy-done | bytes 2072
  7.2 0.0 copy-start.6
  7.2 0.7 %copy-done.6 = s32[8]{0:T(128)S(1)} copy-done((s32[8]{0:T(128)S(1)}, s32[8]{0:T(128)}, u32[]{:S(2)}) %copy-start.6) | copy-done | bytes 56
  7.8 0.0 copy-start.7
  7.8 0.7 %copy-done.7 = s32[8]{0:T(128)S(1)} copy-done((s32[8]{0:T(128)S(1)}, s32[8]{0:T(128)}, u32[]{:S(2)}) %copy-start.7) | copy-done | bytes 56
  8.5 32.0 %replay.1 = (bf16[64,512]{1,0:T(8,128)(2,1)S(1)}, f32[1,64]{1,0:T(1,128)S(1)}) custom-call(s32[8]{0:T(128)S(1)} %copy-done.6, s32[8]{0:T(128)S(1)} %copy-done.7, s32[8,64]{1,0:T(8,128)S(1)} %copy-done.4, s32[8,64]{1,0:T(8,128)S(1)} %copy-done.5, bf16[768,1024]{1,0:T(8,128)(2,1)S(1)} %copy-done.1, bf16[1024,512]{1,0:T(8,128)(2,1)S(1)} %copy-done.2, ...), custom_call_target="tpu_custom_call" | custom-call | tf_op jit(solution)/shard_map/replay/pallas_call | solution.py:318
  40.5 0.6 %copy.12 = bf16[64,512]{1,0:T(8,128)(2,1)} copy(bf16[64,512]{1,0:T(8,128)(2,1)S(1)} %get-tuple-element.8) | data formatting | bytes 131072
  41.2 0.5 %copy.13 = f32[64]{0:T(128)} copy(f32[64]{0:T(128)S(1)} %bitcast.1) | data formatting | bytes 512
Async XLA Ops:
  0.6 1.6 %copy-start = (bf16[1024,1024]{1,0:T(8,128)(2,1)S(1)}, bf16[1024,1024]{1,0:T(8,128)(2,1)}, u32[]{:S(2)}) copy-start(bf16[1024,1024]{1,0:T(8,128)(2,1)} %cat_hbm.1) | copy-start | bytes 6291460
  2.2 1.4 %copy-start.1 = (bf16[768,1024]{1,0:T(8,128)(2,1)S(1)}, bf16[768,1024]{1,0:T(8,128)(2,1)}, u32[]{:S(2)}) copy-start(bf16[768,1024]{1,0:T(8,128)(2,1)} %events_hbm.1) | copy-start | bytes 4718596
  3.6 1.2 %copy-start.2 = (bf16[1024,512]{1,0:T(8,128)(2,1)S(1)}, bf16[1024,512]{1,0:T(8,128)(2,1)}, u32[]{:S(2)}) copy-start(bf16[1024,512]{1,0:T(8,128)(2,1)} %w_hbm.1) | copy-start | bytes 3145732
  4.9 0.9 %copy-start.3 = (bf16[128,1024]{1,0:T(8,128)(2,1)S(1)}, bf16[128,1024]{1,0:T(8,128)(2,1)}, u32[]{:S(2)}) copy-start(bf16[128,1024]{1,0:T(8,128)(2,1)} %w_out_hbm.1) | copy-start | bytes 786436
  5.8 0.7 %copy-start.4 = (s32[8,64]{1,0:T(8,128)S(1)}, s32[8,64]{1,0:T(8,128)}, u32[]{:S(2)}) copy-start(s32[8,64]{1,0:T(8,128)} %positions.1) | copy-start | bytes 6148
  6.5 0.7 %copy-start.5 = (s32[8,64]{1,0:T(8,128)S(1)}, s32[8,64]{1,0:T(8,128)}, u32[]{:S(2)}) copy-start(s32[8,64]{1,0:T(8,128)} %logged.1) | copy-start | bytes 6148
  7.2 0.7 %copy-start.6 = (s32[8]{0:T(128)S(1)}, s32[8]{0:T(128)}, u32[]{:S(2)}) copy-start(s32[8]{0:T(128)} %packing.1) | copy-start | bytes 100
  7.8 0.7 %copy-start.7 = (s32[8]{0:T(128)S(1)}, s32[8]{0:T(128)}, u32[]{:S(2)}) copy-start(s32[8]{0:T(128)} %lengths.1) | copy-start | bytes 100

commit v2 on v1

v2 whole, which is shorter than its diff:
```python
import functools
import math

import jax
import jax.numpy as jnp
from jax import lax
from jax.experimental import pallas as pl
from jax.experimental.pallas import tpu as pltpu
from jax.sharding import PartitionSpec as P

DH = 128
LANES = 128
ITEM_BLOCK = 256
MESH = pl.DeviceIdType.MESH


def silu(x):
    return x / (1.0 + jnp.exp(-x))


def kernel(
    nz,
    nt,
    packing_hbm,
    lengths_hbm,
    positions_hbm,
    logged_hbm,
    events_hbm,
    w_hbm,
    w_out_hbm,
    cat_hbm,
    state_out,
    prop_out,
    packing,
    lengths,
    positions,
    logged,
    events,
    w_vk,
    w_uq,
    w_full,
    cat,
    chosen_all,
    gated_all,
    states,
    ids,
    stage,
    stats,
    load_sem,
    z_send,
    z_recv,
    x_send,
    x_recv,
    sib_send,
    sib_recv,
    w_send,
    w_recv,
    ws_send,
    ws_recv,
    g_send,
    g_recv,
    gs_send,
    gs_recv,
    s_send,
    s_recv,
):
    z = lax.axis_index("item")
    c = lax.axis_index("dp")
    t = lax.axis_index("tensor")
    slot = z * 2 + c
    other = 1 - c
    imps = positions.shape[1]
    rows, width = events.shape
    share = width // nt
    nslots = nz * 2
    nlines = nz * nt
    ndev = nlines * 2
    me = slot * nt + t

    def each_z(first, body):
        if nz <= 4:
            for r in range(first, nz):
                body(r)
        else:
            lax.fori_loop(first, nz, lambda r, carry: (body(r), carry)[1], 0)

    def z_at(r):
        return lax.rem(z + r, nz)

    def z_from(r):
        return lax.rem(z + nz - r, nz)

    def t_at(r):
        return lax.rem(t + r, nt)

    def t_from(r):
        return lax.rem(t + nt - r, nt)

    def each_peer(body):
        for dt in range(nt):
            for dc in range(2):
                each_z(
                    0 if dt or dc else 1,
                    lambda r: body(z_at(r), other if dc else c, t_at(dt)),
                )

    def each_line(body):
        for dt in range(nt):
            each_z(0 if dt else 1, lambda r: body(r, dt))

    def remote(src, dst, send_sem, recv_sem, **device_id):
        return pltpu.make_async_remote_copy(
            src_ref=src,
            dst_ref=dst,
            send_sem=send_sem,
            recv_sem=recv_sem,
            device_id=device_id,
            device_id_type=MESH,
        )

    loads = [
        pltpu.make_async_copy(events_hbm, events, load_sem.at[0]),
        pltpu.make_async_copy(w_hbm.at[:, 0:DH], w_uq.at[:, 0:DH], load_sem.at[1]),
        pltpu.make_async_copy(w_hbm.at[:, 2 * DH : 3 * DH], w_uq.at[:, DH : 2 * DH], load_sem.at[2]),
        pltpu.make_async_copy(w_hbm.at[:, DH : 2 * DH], w_vk.at[:, 0:DH], load_sem.at[3]),
        pltpu.make_async_copy(w_hbm.at[:, 3 * DH : 4 * DH], w_vk.at[:, DH : 2 * DH], load_sem.at[4]),
        pltpu.make_async_copy(w_out_hbm, w_full.at[pl.ds(pl.multiple_of(t * DH, DH), DH), :], load_sem.at[5]),
        pltpu.make_async_copy(cat_hbm, cat, load_sem.at[6]),
    ]
    small = [
        pltpu.make_async_copy(packing_hbm, packing, load_sem.at[7]),
        pltpu.make_async_copy(lengths_hbm, lengths, load_sem.at[8]),
        pltpu.make_async_copy(positions_hbm, positions, load_sem.at[9]),
        pltpu.make_async_copy(logged_hbm, logged, load_sem.at[10]),
    ]
    for copy in small:
        copy.start()
    for copy in loads:
        copy.start()

    barrier = pltpu.get_barrier_semaphore()

    def greet(peer_z, peer_c, peer_t):
        peer = {"item": peer_z, "dp": peer_c, "tensor": peer_t}
        pl.semaphore_signal(barrier, inc=1, device_id=peer, device_id_type=MESH)

    each_peer(greet)

    for copy in small:
        copy.wait()
    hist = packing[slot]
    length = lengths[hist].astype(jnp.float32)
    pos_row = positions[pl.ds(hist, 1), :].astype(jnp.float32)
    eye = lax.broadcasted_iota(jnp.int32, (imps, imps), 0) == lax.broadcasted_iota(
        jnp.int32, (imps, imps), 1
    )
    pos_col = jnp.sum(jnp.where(eye, pos_row, 0.0), axis=1, keepdims=True)
    spots = lax.broadcasted_iota(jnp.int32, (imps, rows), 1).astype(jnp.float32)
    pick = jnp.where(spots == pos_col, 1.0, 0.0).astype(jnp.bfloat16)
    for j in range(nslots):
        ids[0:1, j * imps : (j + 1) * imps] = logged[pl.ds(packing[j], 1), :]

    def rows_of(which):
        return pl.ds(pl.multiple_of(which * imps, imps), imps)

    loads[0].wait()
    chosen = jnp.dot(pick, events[...], preferred_element_type=jnp.float32).astype(jnp.bfloat16)
    chosen_all[rows_of(slot), :] = chosen
    pl.semaphore_wait(barrier, ndev - 1)

    def cols_of(which):
        return pl.ds(pl.multiple_of(which * share, LANES), share)

    def head_cols(which):
        return pl.ds(pl.multiple_of(which * DH, DH), DH)

    def z_copy(r, source_z):
        part = chosen_all.at[rows_of(source_z * 2 + c), cols_of(t)]
        return remote(part, part, z_send.at[r], z_recv.at[r], item=z_at(r))

    def x_copy(r, dt, source_t):
        part = chosen_all.at[rows_of(z_from(r) * 2 + c), cols_of(source_t)]
        k = r * nt + dt
        return remote(part, part, x_send.at[k], x_recv.at[k], tensor=t_at(dt))

    def sib_copy(r, source_c):
        part = chosen_all.at[rows_of(z_from(r) * 2 + source_c), :]
        return remote(part, part, sib_send.at[r], sib_recv.at[r], dp=other)

    half = DH // 2

    def w_rows(source_t, source_c):
        return w_full.at[pl.ds(pl.multiple_of(source_t * DH + source_c * half, half), half), :]

    def w_copy(dt, source_t):
        part = w_out_hbm.at[pl.ds(pl.multiple_of(c * half, half), half), :]
        return remote(
            part, w_rows(source_t, c), w_send.at[dt], w_recv.at[dt], tensor=t_at(dt)
        )

    def ws_copy(dt, source_c):
        part = w_rows(t_from(dt), source_c)
        return remote(part, part, ws_send.at[dt], ws_recv.at[dt], dp=other)

    def gated_at(source_z, source_c, source_t):
        return gated_all.at[rows_of(source_z * 2 + source_c), head_cols(source_t)]

    def g_copy(r, dt, source_z, source_t):
        part = gated_at(source_z, c, source_t)
        k = r * nt + dt
        return remote(part, part, g_send.at[k], g_recv.at[k], item=z_at(r), tensor=t_at(dt))

    def gs_copy(r, dt):
        part = gated_at(z_from(r), c, t_from(dt))
        return remote(part, part, gs_send.at[r * nt + dt], gs_recv, dp=other)

    each_z(1, lambda r: z_copy(r, z).start())
    for dt in range(1, nt):
        w_copy(dt, t).start()
    sib_copy(0, c).start()

    loads[1].wait()
    loads[2].wait()
    gate_query = silu(
        jnp.dot(chosen, w_uq[...], preferred_element_type=jnp.float32)
    ).astype(jnp.bfloat16)
    loads[3].wait()
    loads[4].wait()
    values_keys = silu(
        jnp.dot(events[...], w_vk[...], preferred_element_type=jnp.float32)
    ).astype(jnp.bfloat16)
    scores = lax.dot_general(
        gate_query[:, DH:],
        values_keys[:, DH:],
        (((1,), (1,)), ((), ())),
        preferred_element_type=jnp.float32,
    ) * (1.0 / math.sqrt(DH))
    is_valid = (spots <= pos_col) & (spots < length)
    weights = jnp.where(is_valid, silu(scores), 0.0).astype(jnp.bfloat16)
    attended = jnp.dot(weights, values_keys[:, :DH], preferred_element_type=jnp.float32)
    inverse = lax.rsqrt(jnp.mean(attended * attended, axis=-1, keepdims=True) + 1e-06)
    gated = (attended * inverse * gate_query[:, :DH].astype(jnp.float32)).astype(jnp.bfloat16)
    gated_all[rows_of(slot), head_cols(t)] = gated

    each_line(lambda r, dt: g_copy(r, dt, z, t).start())
    gs_copy(0, 0).start()
    for dt in range(1, nt):
        w_copy(dt, t_from(dt)).wait_recv()
        ws_copy(dt, c).start()

    def pass_across(r):
        z_copy(r, z_from(r)).wait_recv()
        for dt in range(1, nt):
            x_copy(r, dt, t).start()

    each_z(1, pass_across)

    def pass_gated(r, dt):
        g_copy(r, dt, z_from(r), t_from(dt)).wait_recv()
        gs_copy(r, dt).start()

    each_line(pass_gated)

    def pass_chosen(r):
        for dt in range(1, nt):
            x_copy(r, dt, t_from(dt)).wait_recv()
        sib_copy(r, c).start()

    each_z(1, pass_chosen)

    loads[5].wait()
    loads[6].wait()
    for dt in range(1, nt):
        ws_copy(dt, other).wait_recv()
    arrived = gated_all.at[0 : nz * imps, :]
    remote(arrived, arrived, gs_send.at[0], gs_recv, dp=other).wait_recv()
    each_z(0, lambda r: sib_copy(r, other).wait_recv())

    states[...] = (
        jnp.dot(gated_all[...], w_full[...], preferred_element_type=jnp.float32)
        + chosen_all[...].astype(jnp.float32)
    ).astype(jnp.bfloat16)
    state_out[...] = states[rows_of(slot), cols_of(t)]

    items = cat.shape[0]
    item_ids = ids[...]

    def block(b, carry):
        totals, target = carry
        logits = lax.dot_general(
            cat[pl.ds(pl.multiple_of(b * ITEM_BLOCK, ITEM_BLOCK), ITEM_BLOCK), :],
            states[...],
            (((1,), (1,)), ((), ())),
            preferred_element_type=jnp.float32,
        )
        local = item_ids - (me * items + b * ITEM_BLOCK)
        matches = lax.broadcasted_iota(jnp.int32, logits.shape, 0) == local
        totals = totals + jnp.sum(jnp.exp(logits), axis=0, keepdims=True)
        target = target + jnp.sum(jnp.where(matches, logits, 0.0), axis=0, keepdims=True)
        return totals, target

    zero = jnp.zeros((1, nslots * imps), jnp.float32)
    totals, target = lax.fori_loop(0, items // ITEM_BLOCK, block, (zero, zero))
    upper = lax.broadcasted_iota(jnp.int32, (8, LANES), 0) < 4
    for j in range(nz):
        cut = slice(j * LANES, (j + 1) * LANES)
        stage[j] = jnp.where(upper, totals[:, cut], target[:, cut])

    def s_copy(peer_z, peer_c, peer_t):
        remote(
            stage.at[peer_z], stats.at[me], s_send, s_recv, item=peer_z, dp=peer_c, tensor=peer_t
        ).start()

    each_peer(s_copy)
    stats[me] = stage[z]

    each_z(1, lambda r: z_copy(r, z).wait_send())
    each_z(0, lambda r: sib_copy(r, c).wait_send())
    for dt in range(1, nt):
        w_copy(dt, t).wait_send()
        ws_copy(dt, c).wait_send()
        each_z(1, lambda r: x_copy(r, dt, t).wait_send())
    each_line(lambda r, dt: g_copy(r, dt, z, t).wait_send())
    each_z(0, lambda r: [gs_copy(r, dt).wait_send() for dt in range(nt)])
    others = stats.at[0 : ndev - 1]
    all_stats = remote(others, others, s_send, s_recv, dp=other)
    all_stats.wait_recv()
    whole = jnp.sum(stats[...], axis=0)
    prop = whole[4:5, :] - jnp.log(whole[0:1, :])
    prop = jnp.where(c == 0, prop, pltpu.roll(prop, LANES - imps, 1))
    prop_out[...] = prop[:, :imps]
    all_stats.wait_send()


def local(events, lengths, packing, positions, logged, w_uvqk, w_out, catalogue):
    rows, width = events.shape
    imps = positions.shape[1]
    nz = lax.axis_size("item")
    nt = lax.axis_size("tensor")
    nslots = nz * 2
    ndev = nslots * nt
    items = catalogue.shape[0]
    total_imps = nslots * imps
    dma = pltpu.SemaphoreType.DMA
    vmem = pl.BlockSpec(memory_space=pltpu.VMEM)
    hbm = pl.BlockSpec(memory_space=pltpu.HBM)
    state, prop = pl.pallas_call(
        functools.partial(kernel, nz, nt),
        out_shape=(
            jax.ShapeDtypeStruct((imps, width // nt), jnp.bfloat16),
            jax.ShapeDtypeStruct((1, imps), jnp.float32),
        ),
        in_specs=[hbm] * 8,
        out_specs=(vmem, vmem),
        scratch_shapes=[
            pltpu.SMEM(packing.shape, jnp.int32),
            pltpu.SMEM(lengths.shape, jnp.int32),
            pltpu.VMEM(positions.shape, jnp.int32),
            pltpu.VMEM(logged.shape, jnp.int32),
            pltpu.VMEM((rows, width), jnp.bfloat16),
            pltpu.VMEM((width, 2 * DH), jnp.bfloat16),
            pltpu.VMEM((width, 2 * DH), jnp.bfloat16),
            pltpu.VMEM((nt * DH, width), jnp.bfloat16),
            pltpu.VMEM((items, width), jnp.bfloat16),
            pltpu.VMEM((total_imps, width), jnp.bfloat16),
            pltpu.VMEM((total_imps, nt * DH), jnp.bfloat16),
            pltpu.VMEM((total_imps, width), jnp.bfloat16),
            pltpu.VMEM((1, total_imps), jnp.int32),
            pltpu.VMEM((nz, 8, LANES), jnp.float32),
            pltpu.VMEM((ndev, 8, LANES), jnp.float32),
            dma((11,)),
            dma((nz,)),
            dma((nz,)),
            dma((nz * nt,)),
            dma((nz * nt,)),
            dma((nz,)),
            dma((nz,)),
            dma((nt,)),
            dma((nt,)),
            dma((nt,)),
            dma((nt,)),
            dma((nz * nt,)),
            dma((nz * nt,)),
            dma((nz * nt,)),
            dma,
            dma,
            dma,
        ],
        compiler_params=pltpu.CompilerParams(
            collective_id=0, has_side_effects=True, vmem_limit_bytes=63 * 1024 * 1024
        ),
        name="replay",
    )(packing, lengths, positions, logged, events, w_uvqk, w_out, catalogue)
    return state, prop.reshape(imps)


def solution(mesh):
    placed = (
        P(("groups", "item", "dp"), None),
        P("groups"),
        P("groups"),
        P("groups", None),
        P("groups", None),
        P(None, "tensor"),
        P("tensor", None),
        P(("item", "dp", "tensor"), None),
    )
    return jax.shard_map(
        local,
        mesh=mesh,
        in_specs=placed,
        out_specs=(P(("groups", "item", "dp"), "tensor"), P(("groups", "item", "dp"))),
        check_vma=False,
    )
```

time: 42 us -> 32.2 us (0.77)
  local copies, waits for them, and re-layouts: 8.99 us -> 2.59 us
  Pallas kernels: 32 us -> 28.8 us
    unnamed x18 -> x2, local copies, waits for them, and re-layouts: 8.99 us -> 2.59 us
    pallas_call x1, Pallas kernels: 32 us -> 28.8 us  [local(): pl.pallas_call(functools.partial(kernel, nz, nt), out_shape=(jax.ShapeDty...]
where the time goes in v2:
time: 32.2 us; the launch traced here: 32 us
  Pallas kernels  28.8 us (89%)
  local copies, waits for them, and re-layouts  2.59 us (8%)
  between operations  0.64 us (2%)
    pallas_call x1, Pallas kernels, local(): pl.pallas_call(functools.partial(kernel, nz, nt), out_shape=(jax.ShapeDty...  28.8 us
    unnamed x2, local copies, waits for them, and re-layouts  2.59 us

profile of v2, /device:TPU:0, one launch (start us, length us, event | category | flops | bytes accessed | tf_op | source)
XLA Modules:
  0.0 32.0 jit_solution(4432161774354520061)
XLA Ops:
  0.6 28.8 %replay.1 = (bf16[64,512]{1,0:T(8,128)(2,1)}, f32[1,64]{1,0:T(1,128)}) custom-call(s32[8]{0:T(128)} %packing_hbm.1, s32[8]{0:T(128)} %lengths_hbm.1, s32[8,64]{1,0:T(8,128)} %positions_hbm.1, s32[8,64]{1,0:T(8,128)} %logged_hbm.1, bf16[768,1024]{1,0:T(8,128)(2,1)} %events_hbm.1, bf16[1024,512]{1,0:T(8,128)(2,1)} %w_hbm.1, bf16[128,1024]{1,0:T(8,128)(2,1)} %w_out_hbm.1, ...), custom_call_target="tpu_custom_call" | custom-call | tf_op jit(solution)/shard_map/replay/pallas_call | solution.py:347
  29.4 1.5 %copy.12 = bf16[64,512]{1,0:T(8,128)(2,1)} copy(bf16[64,512]{1,0:T(8,128)(2,1)} %get-tuple-element.8) | data formatting | bytes 131072
  30.9 1.1 %copy.13 = f32[64]{0:T(128)} copy(f32[64]{0:T(128)} %bitcast.1) | data formatting | bytes 512

commit v3 on v2

v3 whole, which is shorter than its diff:
```python
import functools
import math

import jax
import jax.numpy as jnp
from jax import lax
from jax.experimental import pallas as pl
from jax.experimental.pallas import tpu as pltpu
from jax.sharding import PartitionSpec as P

DH = 128
LANES = 128
ITEM_BLOCK = 256
MESH = pl.DeviceIdType.MESH


def silu(x):
    return x / (1.0 + jnp.exp(-x))


def kernel(
    nz,
    nt,
    packing_hbm,
    lengths_hbm,
    positions_hbm,
    logged_hbm,
    events_hbm,
    w_hbm,
    w_out_hbm,
    cat_hbm,
    state_out,
    prop_out,
    packing,
    lengths,
    positions,
    logged,
    events,
    w_vk,
    w_uq,
    w_full,
    cat,
    chosen_all,
    gated_all,
    states,
    ids,
    stage,
    stats,
    load_sem,
    z_send,
    z_recv,
    x_send,
    x_recv,
    w_send,
    w_recv,
    ws_send,
    ws_recv,
    g_send,
    g_recv,
    c_send,
    c_recv,
    s_send,
    s_recv,
):
    z = lax.axis_index("item")
    c = lax.axis_index("dp")
    t = lax.axis_index("tensor")
    slot = z * 2 + c
    other = 1 - c
    imps = positions.shape[1]
    rows, width = events.shape
    share = width // nt
    nlines = nz * nt
    line = z * nt + t

    def each_z(first, body, last=nz):
        if nz <= 4:
            for r in range(first, last):
                body(r)
        else:
            lax.fori_loop(first, last, lambda r, carry: (body(r), carry)[1], 0)

    def z_at(r):
        return lax.rem(z + r, nz)

    def z_from(r):
        return lax.rem(z + nz - r, nz)

    def t_at(r):
        return lax.rem(t + r, nt)

    def t_from(r):
        return lax.rem(t + nt - r, nt)

    def each_line(body):
        for dt in range(nt):
            each_z(0 if dt else 1, lambda r: body(r, dt))

    def remote(src, dst, send_sem, recv_sem, **device_id):
        return pltpu.make_async_remote_copy(
            src_ref=src,
            dst_ref=dst,
            send_sem=send_sem,
            recv_sem=recv_sem,
            device_id=device_id,
            device_id_type=MESH,
        )

    loads = [
        pltpu.make_async_copy(events_hbm, events, load_sem.at[0]),
        pltpu.make_async_copy(w_hbm.at[:, 0:DH], w_uq.at[:, 0:DH], load_sem.at[1]),
        pltpu.make_async_copy(w_hbm.at[:, 2 * DH : 3 * DH], w_uq.at[:, DH : 2 * DH], load_sem.at[2]),
        pltpu.make_async_copy(w_hbm.at[:, DH : 2 * DH], w_vk.at[:, 0:DH], load_sem.at[3]),
        pltpu.make_async_copy(w_hbm.at[:, 3 * DH : 4 * DH], w_vk.at[:, DH : 2 * DH], load_sem.at[4]),
        pltpu.make_async_copy(w_out_hbm, w_full.at[pl.ds(pl.multiple_of(t * DH, DH), DH), :], load_sem.at[5]),
        pltpu.make_async_copy(cat_hbm, cat.at[0], load_sem.at[6]),
    ]
    small = [
        pltpu.make_async_copy(packing_hbm, packing, load_sem.at[7]),
        pltpu.make_async_copy(lengths_hbm, lengths, load_sem.at[8]),
        pltpu.make_async_copy(positions_hbm, positions, load_sem.at[9]),
        pltpu.make_async_copy(logged_hbm, logged, load_sem.at[10]),
    ]
    for copy in small:
        copy.start()
    for copy in loads:
        copy.start()

    barrier = pltpu.get_barrier_semaphore()

    def greet(**peer):
        pl.semaphore_signal(barrier, inc=1, device_id=peer, device_id_type=MESH)

    greet(dp=other)
    each_line(lambda r, dt: greet(item=z_at(r), tensor=t_at(dt)))

    for copy in small:
        copy.wait()
    hist = packing[slot]
    length = lengths[hist].astype(jnp.float32)
    pos_row = positions[pl.ds(hist, 1), :].astype(jnp.float32)
    eye = lax.broadcasted_iota(jnp.int32, (imps, imps), 0) == lax.broadcasted_iota(
        jnp.int32, (imps, imps), 1
    )
    pos_col = jnp.sum(jnp.where(eye, pos_row, 0.0), axis=1, keepdims=True)
    spots = lax.broadcasted_iota(jnp.int32, (imps, rows), 1).astype(jnp.float32)
    pick = jnp.where(spots == pos_col, 1.0, 0.0).astype(jnp.bfloat16)
    for r in range(nz):
        ids[0:1, r * imps : (r + 1) * imps] = logged[pl.ds(packing[z_from(r) * 2 + c], 1), :]

    def rows_of(r):
        return pl.ds(r * imps, imps)

    loads[0].wait()
    chosen = jnp.dot(pick, events[...], preferred_element_type=jnp.float32).astype(jnp.bfloat16)
    chosen_all[rows_of(0), :] = chosen

    def cols_of(which):
        return pl.ds(pl.multiple_of(which * share, LANES), share)

    def head_cols(which):
        return pl.ds(pl.multiple_of(which * DH, DH), DH)

    def z_copy(r):
        return remote(
            chosen_all.at[rows_of(0), cols_of(t)],
            chosen_all.at[rows_of(r), cols_of(t)],
            z_send.at[r],
            z_recv.at[r],
            item=z_at(r),
        )

    def x_copy(r, dt, source_t):
        part = chosen_all.at[rows_of(r), cols_of(source_t)]
        k = r * nt + dt
        return remote(part, part, x_send.at[k], x_recv.at[k], tensor=t_at(dt))

    def cat_copy():
        return remote(cat_hbm, cat.at[1], c_send, c_recv, dp=other)

    half = DH // 2

    def w_rows(source_t, source_c):
        return w_full.at[pl.ds(pl.multiple_of(source_t * DH + source_c * half, half), half), :]

    def w_copy(dt, source_t):
        part = w_out_hbm.at[pl.ds(pl.multiple_of(c * half, half), half), :]
        return remote(
            part, w_rows(source_t, c), w_send.at[dt], w_recv.at[dt], tensor=t_at(dt)
        )

    def ws_copy(dt, source_c):
        part = w_rows(t_from(dt), source_c)
        return remote(part, part, ws_send.at[dt], ws_recv.at[dt], dp=other)

    def gated_at(r, source_t):
        return gated_all.at[rows_of(r), head_cols(source_t)]

    def g_copy(r, dt, source_t):
        k = r * nt + dt
        return remote(
            gated_at(0, source_t),
            gated_at(r, source_t),
            g_send.at[k],
            g_recv.at[k],
            item=z_at(r),
            tensor=t_at(dt),
        )

    pl.semaphore_wait(barrier, nlines)
    each_z(1, lambda r: z_copy(r).start())
    for dt in range(1, nt):
        w_copy(dt, t).start()
    cat_copy().start()
    loads[1].wait()
    loads[2].wait()
    gate_query = silu(
        jnp.dot(chosen, w_uq[...], preferred_element_type=jnp.float32)
    ).astype(jnp.bfloat16)
    loads[3].wait()
    loads[4].wait()
    values_keys = silu(
        jnp.dot(events[...], w_vk[...], preferred_element_type=jnp.float32)
    ).astype(jnp.bfloat16)
    scores = lax.dot_general(
        gate_query[:, DH:],
        values_keys[:, DH:],
        (((1,), (1,)), ((), ())),
        preferred_element_type=jnp.float32,
    ) * (1.0 / math.sqrt(DH))
    is_valid = (spots <= pos_col) & (spots < length)
    weights = jnp.where(is_valid, silu(scores), 0.0).astype(jnp.bfloat16)
    attended = jnp.dot(weights, values_keys[:, :DH], preferred_element_type=jnp.float32)
    inverse = lax.rsqrt(jnp.mean(attended * attended, axis=-1, keepdims=True) + 1e-06)
    gated = (attended * inverse * gate_query[:, :DH].astype(jnp.float32)).astype(jnp.bfloat16)

    gated_all[rows_of(0), head_cols(t)] = gated
    each_line(lambda r, dt: g_copy(r, dt, t).start())

    def pass_across(r):
        z_copy(r).wait_recv()
        for dt in range(1, nt):
            x_copy(r, dt, t).start()

    each_z(1, pass_across)
    for dt in range(1, nt):
        w_copy(dt, t_from(dt)).wait_recv()
        ws_copy(dt, c).start()

    each_line(lambda r, dt: g_copy(r, dt, t_from(dt)).wait_recv())
    for dt in range(1, nt):
        ws_copy(dt, other).wait_recv()
    loads[5].wait()

    def take_across(r):
        for dt in range(1, nt):
            x_copy(r, dt, t_from(dt)).wait_recv()

    each_z(1, take_across)
    states[...] = (
        jnp.dot(gated_all[...], w_full[...], preferred_element_type=jnp.float32)
        + chosen_all[...].astype(jnp.float32)
    ).astype(jnp.bfloat16)
    state_out[...] = states[rows_of(0), cols_of(t)]

    items = cat.shape[1]
    item_ids = ids[...]

    def score(shard, source_c, carry):
        base = ((z * 2 + source_c) * nt + t) * items

        def block(b, carry):
            totals, target = carry
            logits = lax.dot_general(
                cat[shard, pl.ds(pl.multiple_of(b * ITEM_BLOCK, ITEM_BLOCK), ITEM_BLOCK), :],
                states[...],
                (((1,), (1,)), ((), ())),
                preferred_element_type=jnp.float32,
            )
            local = item_ids - (base + b * ITEM_BLOCK)
            matches = lax.broadcasted_iota(jnp.int32, logits.shape, 0) == local
            totals = totals + jnp.sum(jnp.exp(logits), axis=0, keepdims=True)
            target = target + jnp.sum(jnp.where(matches, logits, 0.0), axis=0, keepdims=True)
            return totals, target

        return lax.fori_loop(0, items // ITEM_BLOCK, block, carry)

    zero = jnp.zeros((1, nz * imps), jnp.float32)
    loads[6].wait()
    carry = score(0, c, (zero, zero))
    cat_copy().wait_recv()
    totals, target = score(1, other, carry)
    upper = lax.broadcasted_iota(jnp.int32, (8, LANES), 0) < 4
    for r in range(nz):
        cut = slice(r // 2 * LANES, (r // 2 + 1) * LANES)
        tile = jnp.where(upper, totals[:, cut], target[:, cut])
        stage[r] = pltpu.roll(tile, LANES - imps, 1) if r % 2 else tile

    def s_copy(r, dt):
        remote(
            stage.at[r], stats.at[line], s_send, s_recv, item=z_from(r), tensor=t_at(dt)
        ).start()

    each_line(s_copy)
    stats[line] = stage[0]

    each_z(1, lambda r: z_copy(r).wait_send())
    cat_copy().wait_send()
    for dt in range(1, nt):
        w_copy(dt, t).wait_send()
        ws_copy(dt, c).wait_send()
        each_z(1, lambda r: x_copy(r, dt, t).wait_send())
    each_line(lambda r, dt: g_copy(r, dt, t).wait_send())
    others = stats.at[0 : nlines - 1]
    all_stats = remote(others, others, s_send, s_recv, dp=other)
    all_stats.wait_recv()
    whole = jnp.sum(stats[...], axis=0)
    prop = whole[4:5, :] - jnp.log(whole[0:1, :])
    prop_out[...] = prop[:, :imps]
    all_stats.wait_send()


def local(events, lengths, packing, positions, logged, w_uvqk, w_out, catalogue):
    rows, width = events.shape
    imps = positions.shape[1]
    nz = lax.axis_size("item")
    nt = lax.axis_size("tensor")
    items = catalogue.shape[0]
    dma = pltpu.SemaphoreType.DMA
    vmem = pl.BlockSpec(memory_space=pltpu.VMEM)
    hbm = pl.BlockSpec(memory_space=pltpu.HBM)
    state, prop = pl.pallas_call(
        functools.partial(kernel, nz, nt),
        out_shape=(
            jax.ShapeDtypeStruct((imps, width // nt), jnp.bfloat16),
            jax.ShapeDtypeStruct((1, imps), jnp.float32),
        ),
        in_specs=[hbm] * 8,
        out_specs=(vmem, vmem),
        scratch_shapes=[
            pltpu.SMEM(packing.shape, jnp.int32),
            pltpu.SMEM(lengths.shape, jnp.int32),
            pltpu.VMEM(positions.shape, jnp.int32),
            pltpu.VMEM(logged.shape, jnp.int32),
            pltpu.VMEM((rows, width), jnp.bfloat16),
            pltpu.VMEM((width, 2 * DH), jnp.bfloat16),
            pltpu.VMEM((width, 2 * DH), jnp.bfloat16),
            pltpu.VMEM((nt * DH, width), jnp.bfloat16),
            pltpu.VMEM((2, items, width), jnp.bfloat16),
            pltpu.VMEM((nz * imps, width), jnp.bfloat16),
            pltpu.VMEM((nz * imps, nt * DH), jnp.bfloat16),
            pltpu.VMEM((nz * imps, width), jnp.bfloat16),
            pltpu.VMEM((1, nz * imps), jnp.int32),
            pltpu.VMEM((nz, 8, LANES), jnp.float32),
            pltpu.VMEM((nz * nt, 8, LANES), jnp.float32),
            dma((11,)),
            dma((nz,)),
            dma((nz,)),
            dma((nz * nt,)),
            dma((nz * nt,)),
            dma((nt,)),
            dma((nt,)),
            dma((nt,)),
            dma((nt,)),
            dma((nz * nt,)),
            dma((nz * nt,)),
            dma,
            dma,
            dma,
            dma,
        ],
        compiler_params=pltpu.CompilerParams(
            collective_id=0, has_side_effects=True, vmem_limit_bytes=63 * 1024 * 1024
        ),
        name="replay",
    )(packing, lengths, positions, logged, events, w_uvqk, w_out, catalogue)
    return state, prop.reshape(imps)


def solution(mesh):
    placed = (
        P(("groups", "item", "dp"), None),
        P("groups"),
        P("groups"),
        P("groups", None),
        P("groups", None),
        P(None, "tensor"),
        P("tensor", None),
        P(("item", "dp", "tensor"), None),
    )
    return jax.shard_map(
        local,
        mesh=mesh,
        in_specs=placed,
        out_specs=(P(("groups", "item", "dp"), "tensor"), P(("groups", "item", "dp"))),
        check_vma=False,
    )
```

time: 32.2 us -> 31.3 us (0.972)
  Pallas kernels: 28.8 us -> 27.9 us
    pallas_call x1, Pallas kernels: 28.8 us -> 27.9 us  [local(): pl.pallas_call(functools.partial(kernel, nz, nt), out_shape=(jax.ShapeDty...]
where the time goes in v3:
time: 31.3 us; the launch traced here: 31.1 us
  Pallas kernels  27.9 us (89%)
  local copies, waits for them, and re-layouts  2.59 us (8%)
  between operations  0.64 us (2%)
    pallas_call x1, Pallas kernels, local(): pl.pallas_call(functools.partial(kernel, nz, nt), out_shape=(jax.ShapeDty...  27.9 us
    unnamed x2, local copies, waits for them, and re-layouts  2.59 us

profile of v3, /device:TPU:0, one launch (start us, length us, event | category | flops | bytes accessed | tf_op | source)
XLA Modules:
  0.0 31.1 jit_solution(12281700714321916537)
XLA Ops:
  0.6 27.9 %replay.1 = (bf16[64,512]{1,0:T(8,128)(2,1)}, f32[1,64]{1,0:T(1,128)}) custom-call(s32[8]{0:T(128)} %packing_hbm.1, s32[8]{0:T(128)} %lengths_hbm.1, s32[8,64]{1,0:T(8,128)} %positions_hbm.1, s32[8,64]{1,0:T(8,128)} %logged_hbm.1, bf16[768,1024]{1,0:T(8,128)(2,1)} %events_hbm.1, bf16[1024,512]{1,0:T(8,128)(2,1)} %w_hbm.1, bf16[128,1024]{1,0:T(8,128)(2,1)} %w_out_hbm.1, ...), custom_call_target="tpu_custom_call" | custom-call | tf_op jit(solution)/shard_map/replay/pallas_call | solution.py:332
  28.5 1.5 %copy.12 = bf16[64,512]{1,0:T(8,128)(2,1)} copy(bf16[64,512]{1,0:T(8,128)(2,1)} %get-tuple-element.8) | data formatting | bytes 131072
  30.0 1.1 %copy.13 = f32[64]{0:T(128)} copy(f32[64]{0:T(128)} %bitcast.1) | data formatting | bytes 512

commit v4 on v3

--- a/solution.py
+++ b/solution.py
@@ -10,7 +10,7 @@
 
 DH = 128
 LANES = 128
-ITEM_BLOCK = 256
+ITEM_BLOCK = 512
 MESH = pl.DeviceIdType.MESH
 
 
@@ -123,8 +123,7 @@
     ]
     for copy in small:
         copy.start()
-    for copy in loads:
-        copy.start()
+    loads[0].start()
 
     barrier = pltpu.get_barrier_semaphore()
 
@@ -152,6 +151,8 @@
         return pl.ds(r * imps, imps)
 
     loads[0].wait()
+    for copy in loads[1:]:
+        copy.start()
     chosen = jnp.dot(pick, events[...], preferred_element_type=jnp.float32).astype(jnp.bfloat16)
     chosen_all[rows_of(0), :] = chosen
 
@@ -222,6 +223,12 @@
     values_keys = silu(
         jnp.dot(events[...], w_vk[...], preferred_element_type=jnp.float32)
     ).astype(jnp.bfloat16)
+    def pass_across(r):
+        z_copy(r).wait_recv()
+        for dt in range(1, nt):
+            x_copy(r, dt, t).start()
+
+    each_z(1, pass_across)
     scores = lax.dot_general(
         gate_query[:, DH:],
         values_keys[:, DH:],
@@ -237,12 +244,6 @@
     gated_all[rows_of(0), head_cols(t)] = gated
     each_line(lambda r, dt: g_copy(r, dt, t).start())
 
-    def pass_across(r):
-        z_copy(r).wait_recv()
-        for dt in range(1, nt):
-            x_copy(r, dt, t).start()
-
-    each_z(1, pass_across)
     for dt in range(1, nt):
         w_copy(dt, t_from(dt)).wait_recv()
         ws_copy(dt, c).start()

time: 31.3 us -> 29.1 us (0.930)
  Pallas kernels: 27.9 us -> 25.7 us
    pallas_call x1, Pallas kernels: 27.9 us -> 25.7 us  [local(): pl.pallas_call(functools.partial(kernel, nz, nt), out_shape=(jax.ShapeDty...]
where the time goes in v4:
time: 29.1 us; the launch traced here: 28.9 us
  Pallas kernels  25.7 us (88%)
  local copies, waits for them, and re-layouts  2.59 us (9%)
  between operations  0.64 us (2%)
    pallas_call x1, Pallas kernels, local(): pl.pallas_call(functools.partial(kernel, nz, nt), out_shape=(jax.ShapeDty...  25.7 us
    unnamed x2, local copies, waits for them, and re-layouts  2.59 us

profile of v4, /device:TPU:0, one launch (start us, length us, event | category | flops | bytes accessed | tf_op | source)
XLA Modules:
  0.0 28.9 jit_solution(3256362872686654828)
XLA Ops:
  0.6 25.7 %replay.1 = (bf16[64,512]{1,0:T(8,128)(2,1)}, f32[1,64]{1,0:T(1,128)}) custom-call(s32[8]{0:T(128)} %packing_hbm.1, s32[8]{0:T(128)} %lengths_hbm.1, s32[8,64]{1,0:T(8,128)} %positions_hbm.1, s32[8,64]{1,0:T(8,128)} %logged_hbm.1, bf16[768,1024]{1,0:T(8,128)(2,1)} %events_hbm.1, bf16[1024,512]{1,0:T(8,128)(2,1)} %w_hbm.1, bf16[128,1024]{1,0:T(8,128)(2,1)} %w_out_hbm.1, ...), custom_call_target="tpu_custom_call" | custom-call | tf_op jit(solution)/shard_map/replay/pallas_call | solution.py:333
  26.3 1.5 %copy.12 = bf16[64,512]{1,0:T(8,128)(2,1)} copy(bf16[64,512]{1,0:T(8,128)(2,1)} %get-tuple-element.8) | data formatting | bytes 131072
  27.8 1.1 %copy.13 = f32[64]{0:T(128)} copy(f32[64]{0:T(128)} %bitcast.1) | data formatting | bytes 512
